TPU v7x, 128 devices: a whole 4x4x4 slice. The times are simulated.
128 devices in a mesh: sx: 8 (over y, z_lo), sz: 16 (over x, z_hi, core).
Axes of the slice: x: 4, y: 4, z: 4 (z_hi: 2, z_lo: 2; z = z_hi * 2 + z_lo), core: 2. Of those that a mesh axis runs over, the one named last changes fastest.
Arguments:
- right_side: float32 [72, 256, 4096], P('sx', 'sz'), may hold values from -6 to 6
- coupling: bfloat16 [72, 5, 256, 256], P('sx'), may hold values from -0.15625 to 0.15625
- harmonic_offsets: int32 [5], replicated, may hold values from -6 to 6, as said below
- eigen_basis: bfloat16 [256, 256], replicated, may hold values from -0.375 to 0.375
- eigen_inverse: bfloat16 [256, 256], replicated, may hold values from -0.375 to 0.375
- eigen_size: float32 [256], replicated, may hold values from 0.5 to 50
Outputs:
- solution: float32 [72, 256, 4096], P('sx', 'sz')
Inputs may be any that keep to these rules, and one draw needn't show every extreme that they name: `harmonic_offsets`: the offsets are distinct; some offset equals 6 and some equals -6.
All inputs are finite; a program needn't handle non-finite values.
Results may differ from a plain program's by a relative error of at most 0.00065.
The roundings to bfloat16 on the way count: a program that leaves them out, or rounds other values in their place, can miss the bound.
Values may be sent and summed in bfloat16 or wider, within the bound.
A program may use at most 128 MiB of HBM per device.

v0:
```python
import jax
import jax.numpy as jnp
from jax import lax
from jax.sharding import PartitionSpec as P

KX = 72
KZ = 128
H = 5
OFF = 6
STEPS = 2
R = 32


def extended(value, sides, width):
    for axis, dim in sides:
        peers, length = (lax.axis_size(axis), value.shape[dim])
        up = [(i, (i + 1) % peers) for i in range(peers)]
        down = [(j, i) for i, j in up]
        last = lax.slice_in_dim(value, length - width, length, axis=dim)
        first = lax.slice_in_dim(value, 0, width, axis=dim)
        before = lax.ppermute(last, axis, up)
        after = lax.ppermute(first, axis, down)
        value = jnp.concatenate([before, value, after], axis=dim)
    return value


def wave_table(mode_count, span_count):
    first_mode = lax.axis_index("sx") * mode_count
    first_span = lax.axis_index("sz") * span_count
    modes = first_mode + jnp.arange(mode_count, dtype=jnp.int32)
    spans = first_span + jnp.arange(span_count, dtype=jnp.int32)
    signed_x = jnp.where(modes < KX // 2, modes, modes - KX).astype(jnp.float32) * (4.0 / KX)
    signed_z = jnp.where(spans < KZ // 2, spans, spans - KZ).astype(jnp.float32) * (4.0 / KZ)
    table = 1.0 + signed_x[:, None] ** 2 + signed_z[None, :] ** 2
    return jnp.repeat(table, R, axis=1)


def precondition(residual, eigen_basis, eigen_inverse, eigen_size, wave_square):
    rounded = residual.astype(jnp.bfloat16)
    spectral = jnp.einsum("ij,kjc->kic", eigen_inverse, rounded, preferred_element_type=jnp.float32)
    factor = -1.0 / (eigen_size[None, :, None] + wave_square[:, None, :])
    scaled = (spectral * factor).astype(jnp.bfloat16)
    result = jnp.einsum("ij,kjc->kic", eigen_basis, scaled, preferred_element_type=jnp.float32)
    return result.astype(jnp.bfloat16)


def apply_operator(search, coupling, harmonic_offsets, wave_square):
    mode_count = search.shape[0]
    padded = extended(search, (("sx", 0),), OFF)
    accum = -wave_square[:, None, :] * search.astype(jnp.float32)
    for harmonic in range(H):
        source = lax.dynamic_slice_in_dim(padded, OFF + harmonic_offsets[harmonic], mode_count, 0)
        accum = accum + jnp.einsum(
            "kij,kjc->kic", coupling[:, harmonic], source, preferred_element_type=jnp.float32
        )
    return accum


def relax(solution, residual, search_full, image):
    inner = jnp.sum(jnp.sum(image * residual, axis=(0, 1)).reshape(-1, R), axis=0)
    energy = jnp.sum(jnp.sum(image * image, axis=(0, 1)).reshape(-1, R), axis=0)
    aligned, total_energy = lax.psum((inner, energy), ("sx", "sz"))
    step_size = jnp.tile(aligned / (total_energy + 1e-06), image.shape[2] // R)
    return (solution + step_size * search_full, residual - step_size * image)


def shards(right_side, coupling, harmonic_offsets, eigen_basis, eigen_inverse, eigen_size):
    residual = lax.all_to_all(right_side, "sz", split_axis=2, concat_axis=1, tiled=True)
    wave_square = wave_table(residual.shape[0], residual.shape[2] // R)
    solution = jnp.zeros_like(residual)
    for sweep in range(STEPS):
        search = precondition(residual, eigen_basis, eigen_inverse, eigen_size, wave_square)
        image = apply_operator(search, coupling, harmonic_offsets, wave_square)
        solution, residual = relax(solution, residual, search.astype(jnp.float32), image)
    return lax.all_to_all(solution, "sz", split_axis=1, concat_axis=2, tiled=True)


def solution(mesh):
    in_specs = (P("sx", "sz", None), P("sx", None, None, None), P(), P(), P(), P())
    out_specs = P("sx", "sz", None)
    return jax.shard_map(shards, mesh=mesh, in_specs=in_specs, out_specs=out_specs, check_vma=False)
```

profile of v0, /device:TPU:1, one launch (start us, length us, event | category | flops | bytes accessed | tf_op | source)
XLA Modules:
  0.0 424.5 jit_solution(962264210277215487)
XLA Ops:
  0.0 0.0 copy-start
  0.0 17.6 %copy.68 = f32[9,16,4096]{1,0,2:T(8,128)} copy(f32[9,16,4096]{2,1,0:T(8,128)} %param.6) | data formatting | bytes 4718592 | tf_op args[0]
  17.6 19.3 %reshape.75 = f32[16,1,36864]{2,1,0:T(1,128)} reshape(f32[4096,9,16]{2,1,0:T(8,128)} %bitcast.113) | data formatting | bytes 4718592
  36.9 9.1 %all-to-all-start = ((f32[16,1,36864]{2,1,0:T(1,128)}), f32[16,1,36864]{2,1,0:T(1,128)S(1)}, u32[]{:S(2)}, u32[]{:S(2)}) async-start(f32[16,1,36864]{2,1,0:T(1,128)} %reshape.75), calls=%async_computation | async-start | bytes 4718592 | tf_op jit(solution)/shard_map/all_to_all | solution.py:68
  46.1 0.1 broadcast_add_fusion
  46.1 0.1 broadcast_in_dim.2
  46.2 0.1 broadcast_in_dim_reshape.2
  46.3 31.0 %all-to-all-done = f32[16,1,36864]{2,1,0:T(1,128)S(1)} async-done(((f32[16,1,36864]{2,1,0:T(1,128)}), f32[16,1,36864]{2,1,0:T(1,128)S(1)}, u32[]{:S(2)}, u32[]{:S(2)}) %all-to-all-start) | async-done | bytes 2359328 | tf_op jit(solution)/shard_map/all_to_all | solution.py:68
  77.3 1.4 copy-done.4
  78.7 0.6 broadcast.95
  79.3 8.0 %reduce = f32[16,36864]{1,0:T(8,128)S(1)} reduce(f32[16,1,36864]{2,1,0:T(1,128)} %copy-done.4, f32[]{:T(128)} %broadcast.95), dimensions={1}, to_apply=%all_to_all.26.reduce_sub_computation | reduce | bytes 4718596 | tf_op jit(solution)/shard_map/all_to_all | solution.py:68
  87.3 21.2 %reshape.76 = f32[4096,9,16]{2,1,0:T(8,128)} reshape(f32[16,36864]{1,0:T(8,128)S(1)} %reduce) | data formatting | bytes 4718592
  108.5 18.9 %copy.70 = f32[9,16,16,256]{3,2,1,0:T(8,128)S(1)} copy(f32[9,16,16,256]{2,0,3,1:T(8,128)} %bitcast.112) | data formatting | bytes 4718592 | tf_op jit(solution)/shard_map/all_to_all | solution.py:68
  127.4 0.0 copy-start.7
  127.4 1.5 copy.71
  128.9 0.0 copy-done
  128.9 0.0 copy-done.6
  128.9 3.3 fusion.13
  132.2 2.4 fusion.89
  134.6 0.7 collective-permute-start
  135.3 2.8 collective-permute-start.1
  138.1 0.7 fusion.90
  145.0 23.4 %collective-permute-done = bf16[6,256,256]{2,1,0:T(8,128)(2,1)} collective-permute-done((bf16[6,256,256]{2,1,0:T(8,128)(2,1)}, bf16[6,256,256]{2,1,0:T(8,128)(2,1)}, u32[]{:S(2)}, u32[]{:S(2)}) %collective-permute-start) | collective-permute-done | bytes 786464 | tf_op jit(solution)/shard_map/ppermute | solution.py:21
  168.4 2.3 collective-permute-done.1
  170.7 2.2 pad_maximum_fusion
  172.9 0.0 slice-start.1
  172.9 1.9 fusion.21
  174.8 1.8 fusion.25
  176.5 0.0 slice-done
  176.5 0.0 slice-done.1
  176.6 0.5 fusion.29
  177.0 0.0 copy-start.1
  177.0 0.5 fusion.17
  177.5 0.8 copy-done.1
  178.3 2.7 multiply_reduce_fusion.2
  181.0 0.1 reshape.69
  181.1 0.1 reshape.70
  181.2 67.8 %all-reduce.1 = (f32[32]{0:T(128)S(1)}, f32[32]{0:T(128)S(1)}) all-reduce(f32[32]{0:T(128)S(1)} %reduce_sum.73, f32[32]{0:T(128)S(1)} %reduce_sum.75), channel_id=1, replica_groups=mesh['sx'=8,'sz'=16] {'sx','sz'}, use_global_device_ids=true, to_apply=%region_2.3 | all-reduce | flops 64 | bytes 512 | tf_op jit(solution)/shard_map/psum | solution.py:62
  249.0 0.1 mul.87
  249.1 3.8 fusion.14
  252.9 1.6 fusion.88
  254.5 0.3 collective-permute-start.2
  254.8 3.3 collective-permute-start.3
  258.2 29.7 %collective-permute-done.2 = bf16[6,256,256]{2,1,0:T(8,128)(2,1)S(1)} collective-permute-done((bf16[6,256,256]{2,1,0:T(8,128)(2,1)S(1)}, bf16[6,256,256]{2,1,0:T(8,128)(2,1)S(1)}, u32[]{:S(2)}, u32[]{:S(2)}) %collective-permute-start.2) | collective-permute-done | bytes 786464 | tf_op jit(solution)/shard_map/ppermute | solution.py:21
  287.9 1.9 collective-permute-done.3
  289.8 1.6 pad_maximum_fusion.1
  291.4 1.8 fusion.23
  293.2 0.5 fusion.27
  293.7 0.5 fusion.31
  294.1 0.0 copy-start.2
  294.1 0.0 copy-start.3
  294.2 0.5 fusion.19
  294.6 0.8 copy-done.2
  295.4 0.8 copy-done.3
  296.2 1.5 multiply_reduce_fusion
  297.7 0.1 reshape.71
  297.8 0.1 reshape.72
  297.9 65.3 %all-reduce = (f32[32]{0:T(128)S(1)}, f32[32]{0:T(128)S(1)}) all-reduce(f32[32]{0:T(128)S(1)} %reduce_sum.77, f32[32]{0:T(128)S(1)} %reduce_sum.79), channel_id=1, replica_groups=mesh['sx'=8,'sz'=16] {'sx','sz'}, use_global_device_ids=true, to_apply=%region_8.9 | all-reduce | flops 64 | bytes 512 | tf_op jit(solution)/shard_map/psum | solution.py:62
  363.2 0.1 mul.95
  363.3 2.0 fusion.5
  365.3 1.5 copy.80
  366.8 54.6 %all_to_all.36 = f32[9,256,256]{2,0,1:T(8,128)S(1)} all-to-all(f32[9,256,256]{2,0,1:T(8,128)S(1)} %copy.80), channel_id=1, replica_groups=mesh['sx'=8,'sz'=16] {'sz'}, dimensions={1} | all-to-all | bytes 4718592 | tf_op jit(solution)/shard_map/all_to_all | solution.py:75
  421.5 1.4 copy.81
  422.8 1.6 all_to_all.33
  (23 shorter events, 0.1 us)
Async XLA Ops:
  0.0 128.9 %copy-start = (bf16[256,256]{1,0:T(8,128)(2,1)S(1)}, bf16[256,256]{1,0:T(8,128)(2,1)}, u32[]{:S(2)}) copy-start(bf16[256,256]{1,0:T(8,128)(2,1)} %param.9) | copy-start | bytes 393220
  36.9 40.4 %all-to-all-start = ((f32[16,1,36864]{2,1,0:T(1,128)}), f32[16,1,36864]{2,1,0:T(1,128)S(1)}, u32[]{:S(2)}, u32[]{:S(2)}) async-start(f32[16,1,36864]{2,1,0:T(1,128)} %reshape.75), calls=%async_computation | async-start | bytes 4718592 | tf_op jit(solution)/shard_map/all_to_all | solution.py:68
  77.3 1.4 copy-start.4
  127.4 1.5 copy-start.6
  127.4 1.5 copy-start.7
  132.2 5.9 %copy-start.5 = (s32[5]{0:T(128)S(1)}, s32[5]{0:T(128)}, u32[]{:S(2)}) copy-start(s32[5]{0:T(128)} %param.8) | copy-start | bytes 64
  134.6 33.8 %collective-permute-start = (bf16[6,256,256]{2,1,0:T(8,128)(2,1)}, bf16[6,256,256]{2,1,0:T(8,128)(2,1)}, u32[]{:S(2)}, u32[]{:S(2)}) collective-permute-start(bf16[6,256,256]{2,1,0:T(8,128)(2,1)} %get-tuple-element.15), channel_id=1, source_target_pairs={{0,16},{16,32},{32,48},{48,64},{64,80},{80,96},{96,112},{112,0},{1... | collective-permute-start | bytes 2359304 | tf_op jit(solution)/shard_map/ppermute | solution.py:21
  135.3 35.4 %collective-permute-start.1 = (bf16[6,256,256]{2,1,0:T(8,128)(2,1)S(1)}, bf16[6,256,256]{2,1,0:T(8,128)(2,1)}, u32[]{:S(2)}, u32[]{:S(2)}) collective-permute-start(bf16[6,256,256]{2,1,0:T(8,128)(2,1)S(1)} %get-tuple-element.16), channel_id=1, source_target_pairs={{16,0},{32,16},{48,32},{64,48},{80,64},{96,80},{112,96},{0,112},{1... | collective-permute-start | bytes 2359304 | tf_op jit(solution)/shard_map/ppermute | solution.py:22
  170.7 5.9 %slice-start = ((s8[5898240]{0:T(1024)(128)(4,1)}), s8[4194304]{0:T(1024)(128)(4,1)S(1)}, s32[]{:S(2)}) async-start(s8[5898240]{0:T(1024)(128)(4,1)} %bitcast.116), calls=%async_computation.2 | async-start | bytes 8388608
  172.9 3.7 slice-start.1
  177.0 1.3 copy-start.1
  252.9 40.3 %slice-start.2 = ((s8[5898240]{0:T(1024)(128)(4,1)}), s8[4194304]{0:T(1024)(128)(4,1)S(1)}, s32[]{:S(2)}) async-start(s8[5898240]{0:T(1024)(128)(4,1)} %bitcast.118), calls=%async_computation.4 | async-start | bytes 8388608
  254.5 33.4 %collective-permute-start.2 = (bf16[6,256,256]{2,1,0:T(8,128)(2,1)S(1)}, bf16[6,256,256]{2,1,0:T(8,128)(2,1)S(1)}, u32[]{:S(2)}, u32[]{:S(2)}) collective-permute-start(bf16[6,256,256]{2,1,0:T(8,128)(2,1)S(1)} %get-tuple-element.13), channel_id=1, source_target_pairs={{0,16},{16,32},{32,48},{48,64},{64,80},{80,96},{96,112},{112,0},{1... | collective-permute-start | bytes 2359304 | tf_op jit(solution)/shard_map/ppermute | solution.py:21
  254.8 38.3 %slice-start.3 = ((s8[5898240]{0:T(1024)(128)(4,1)}), s8[1703936]{0:T(1024)(128)(4,1)S(1)}, s32[]{:S(2)}) async-start(s8[5898240]{0:T(1024)(128)(4,1)} %bitcast.118), calls=%async_computation.5 | async-start | bytes 3407872
  254.8 35.0 %collective-permute-start.3 = (bf16[6,256,256]{2,1,0:T(8,128)(2,1)S(1)}, bf16[6,256,256]{2,1,0:T(8,128)(2,1)S(1)}, u32[]{:S(2)}, u32[]{:S(2)}) collective-permute-start(bf16[6,256,256]{2,1,0:T(8,128)(2,1)S(1)} %get-tuple-element.14), channel_id=1, source_target_pairs={{16,0},{32,16},{48,32},{64,48},{80,64},{96,80},{112,96},{0,112},{1... | collective-permute-start | bytes 2359304 | tf_op jit(solution)/shard_map/ppermute | solution.py:22
  294.1 1.3 copy-start.2
  294.1 2.0 copy-start.3
where the time goes:
time: 426 us; the launch traced here: 424 us
  blocking collectives  188 us (44%)
  local copies, waits for them, and re-layouts  92.6 us (22%)
  waiting for transfers between devices  88.3 us (21%)
  matrix products  19.1 us (4%)
  starting transfers between devices  16.3 us (4%)
  other arithmetic  13.9 us (3%)
  between operations  6.39 us (2%)
    psum x2, blocking collectives, relax(): aligned, total_energy = lax.psum((inner, energy), ('sx', 'sz'))  133 us
    unnamed x27, local copies, waits for them, and re-layouts  61.9 us
    all_to_all x1, blocking collectives, shards(): lax.all_to_all(solution, 'sz', split_axis=1, concat_axis=2, tiled=True)  54.6 us
    ppermute x2, waiting for transfers between devices, extended(): before = lax.ppermute(last, axis, up)  53.1 us
    all_to_all x1, waiting for transfers between devices, shards(): lax.all_to_all(right_side, 'sz', split_axis=2, concat_axis=1, tiled=True)  31 us
    all_to_all x3, local copies, waits for them, and re-layouts, shards(): lax.all_to_all(right_side, 'sz', split_axis=2, concat_axis=1, tiled=True)  21 us
    dot_general x10, matrix products, apply_operator(): jnp.einsum('kij,kjc->kic', coupling[:, harmonic], source, preferred_eleme...  12 us
    all_to_all x1, starting transfers between devices, shards(): lax.all_to_all(right_side, 'sz', split_axis=2, concat_axis=1, tiled=True)  9.13 us
  transfers between devices with their start and end apart: 5, of which 5 were waited for; matrix products, arithmetic and copies ran while one was open for 0% of the time, Pallas kernels for 0%

commit v1 on v0

--- a/solution.py
+++ b/solution.py
@@ -72,7 +72,10 @@
         search = precondition(residual, eigen_basis, eigen_inverse, eigen_size, wave_square)
         image = apply_operator(search, coupling, harmonic_offsets, wave_square)
         solution, residual = relax(solution, residual, search.astype(jnp.float32), image)
-    return lax.all_to_all(solution, "sz", split_axis=1, concat_axis=2, tiled=True)
+    return jnp.concatenate(
+        lax.all_to_all(jnp.stack(jnp.split(solution, lax.axis_size("sz"), axis=1)), "sz", 0, 0),
+        axis=2,
+    )
 
 
 def solution(mesh):

time: 426 us -> 404 us (0.948)
  blocking collectives: 188 us -> 168 us
    all_to_all x1, blocking collectives: 54.6 us -> 35.6 us  [shards(): lax.all_to_all(jnp.stack(jnp.split(solution, lax.axis_size('sz'), axis=1)...]
    unnamed x27 -> x42, local copies, waits for them, and re-layouts: 61.9 us -> 62.1 us
where the time goes in v1:
time: 404 us; the launch traced here: 403 us
  blocking collectives  168 us (42%)
  local copies, waits for them, and re-layouts  90 us (22%)
  waiting for transfers between devices  88.3 us (22%)
  matrix products  19.1 us (5%)
  starting transfers between devices  16.3 us (4%)
  other arithmetic  13.9 us (3%)
  between operations  6.5 us (2%)
    psum x2, blocking collectives, relax(): aligned, total_energy = lax.psum((inner, energy), ('sx', 'sz'))  133 us
    unnamed x42, local copies, waits for them, and re-layouts  62.1 us
    ppermute x2, waiting for transfers between devices, extended(): before = lax.ppermute(last, axis, up)  53.1 us
    all_to_all x1, blocking collectives, shards(): lax.all_to_all(jnp.stack(jnp.split(solution, lax.axis_size('sz'), axis=1)...  35.6 us
    all_to_all x1, waiting for transfers between devices, shards(): lax.all_to_all(right_side, 'sz', split_axis=2, concat_axis=1, tiled=True)  31 us
    all_to_all x3, local copies, waits for them, and re-layouts, shards(): lax.all_to_all(right_side, 'sz', split_axis=2, concat_axis=1, tiled=True)  21 us
    dot_general x10, matrix products, apply_operator(): jnp.einsum('kij,kjc->kic', coupling[:, harmonic], source, preferred_eleme...  12 us
    all_to_all x1, starting transfers between devices, shards(): lax.all_to_all(right_side, 'sz', split_axis=2, concat_axis=1, tiled=True)  9.13 us
  transfers between devices with their start and end apart: 5, of which 5 were waited for; matrix products, arithmetic and copies ran while one was open for 0% of the time, Pallas kernels for 0%

profile of v1, /device:TPU:1, one launch (start us, length us, event | category | flops | bytes accessed | tf_op | source)
XLA Modules:
  0.0 402.6 jit_solution(11718282327919072717)
XLA Ops:
  0.0 0.0 copy-start
  0.0 17.6 %copy.76 = f32[9,16,4096]{1,0,2:T(8,128)} copy(f32[9,16,4096]{2,1,0:T(8,128)} %param.6) | data formatting | bytes 4718592 | tf_op args[0]
  17.6 19.3 %reshape.83 = f32[16,1,36864]{2,1,0:T(1,128)} reshape(f32[4096,9,16]{2,1,0:T(8,128)} %bitcast.175) | data formatting | bytes 4718592
  36.9 9.1 %all-to-all-start = ((f32[16,1,36864]{2,1,0:T(1,128)}), f32[16,1,36864]{2,1,0:T(1,128)S(1)}, u32[]{:S(2)}, u32[]{:S(2)}) async-start(f32[16,1,36864]{2,1,0:T(1,128)} %reshape.83), calls=%async_computation | async-start | bytes 4718592 | tf_op jit(solution)/shard_map/all_to_all | solution.py:68
  46.1 0.1 broadcast_add_fusion
  46.1 0.1 broadcast_in_dim.2
  46.2 0.1 broadcast_in_dim_reshape.2
  46.3 31.0 %all-to-all-done = f32[16,1,36864]{2,1,0:T(1,128)S(1)} async-done(((f32[16,1,36864]{2,1,0:T(1,128)}), f32[16,1,36864]{2,1,0:T(1,128)S(1)}, u32[]{:S(2)}, u32[]{:S(2)}) %all-to-all-start) | async-done | bytes 2359328 | tf_op jit(solution)/shard_map/all_to_all | solution.py:68
  77.3 1.4 copy-done.4
  78.7 0.6 broadcast.95
  79.3 8.0 %reduce = f32[16,36864]{1,0:T(8,128)S(1)} reduce(f32[16,1,36864]{2,1,0:T(1,128)} %copy-done.4, f32[]{:T(128)} %broadcast.95), dimensions={1}, to_apply=%all_to_all.16.reduce_sub_computation | reduce | bytes 4718596 | tf_op jit(solution)/shard_map/all_to_all | solution.py:68
  87.3 21.2 %reshape.84 = f32[4096,9,16]{2,1,0:T(8,128)} reshape(f32[16,36864]{1,0:T(8,128)S(1)} %reduce) | data formatting | bytes 4718592
  108.5 18.9 %copy.78 = f32[9,16,16,256]{3,2,1,0:T(8,128)S(1)} copy(f32[9,16,16,256]{2,0,3,1:T(8,128)} %bitcast.174) | data formatting | bytes 4718592 | tf_op jit(solution)/shard_map/all_to_all | solution.py:68
  127.4 0.0 copy-start.7
  127.4 1.5 copy.79
  128.9 0.0 copy-done
  128.9 0.0 copy-done.6
  128.9 0.0 copy-done.7
  128.9 3.3 fusion.13
  132.2 2.4 fusion.105
  134.6 0.7 collective-permute-start
  135.3 2.8 collective-permute-start.1
  138.1 0.0 copy-done.5
  138.1 0.7 fusion.106
  145.0 23.4 %collective-permute-done = bf16[6,256,256]{2,1,0:T(8,128)(2,1)} collective-permute-done((bf16[6,256,256]{2,1,0:T(8,128)(2,1)}, bf16[6,256,256]{2,1,0:T(8,128)(2,1)}, u32[]{:S(2)}, u32[]{:S(2)}) %collective-permute-start) | collective-permute-done | bytes 786464 | tf_op jit(solution)/shard_map/ppermute | solution.py:21
  168.4 2.3 collective-permute-done.1
  170.7 2.2 pad_maximum_fusion
  172.9 0.0 slice-start.1
  172.9 1.9 fusion.21
  174.8 1.8 fusion.25
  176.5 0.0 slice-done
  176.5 0.0 slice-done.1
  176.6 0.5 fusion.29
  177.0 0.0 copy-start.1
  177.0 0.5 fusion.17
  177.5 0.8 copy-done.1
  178.3 2.7 multiply_reduce_fusion.2
  181.0 0.1 reshape.75
  181.1 0.1 reshape.76
  181.2 67.8 %all-reduce.1 = (f32[32]{0:T(128)S(1)}, f32[32]{0:T(128)S(1)}) all-reduce(f32[32]{0:T(128)S(1)} %reduce_sum.73, f32[32]{0:T(128)S(1)} %reduce_sum.75), channel_id=1, replica_groups=mesh['sx'=8,'sz'=16] {'sx','sz'}, use_global_device_ids=true, to_apply=%region_2.3 | all-reduce | flops 64 | bytes 512 | tf_op jit(solution)/shard_map/psum | solution.py:62
  249.0 0.1 mul.87
  249.1 3.8 fusion.14
  252.9 1.6 fusion.104
  254.5 0.3 collective-permute-start.2
  254.8 3.3 collective-permute-start.3
  258.2 29.7 %collective-permute-done.2 = bf16[6,256,256]{2,1,0:T(8,128)(2,1)S(1)} collective-permute-done((bf16[6,256,256]{2,1,0:T(8,128)(2,1)S(1)}, bf16[6,256,256]{2,1,0:T(8,128)(2,1)S(1)}, u32[]{:S(2)}, u32[]{:S(2)}) %collective-permute-start.2) | collective-permute-done | bytes 786464 | tf_op jit(solution)/shard_map/ppermute | solution.py:21
  287.9 1.9 collective-permute-done.3
  289.8 1.6 pad_maximum_fusion.1
  291.4 1.8 fusion.23
  293.2 0.5 fusion.27
  293.7 0.5 fusion.31
  294.1 0.0 copy-start.2
  294.1 0.0 copy-start.3
  294.2 0.5 fusion.19
  294.6 0.8 copy-done.2
  295.4 0.8 copy-done.3
  296.2 1.5 multiply_reduce_fusion
  297.7 0.1 reshape.77
  297.8 0.1 reshape.78
  297.9 65.1 %all-reduce = (f32[32]{0:T(128)S(1)}, f32[32]{0:T(128)S(1)}) all-reduce(f32[32]{0:T(128)S(1)} %reduce_sum.77, f32[32]{0:T(128)S(1)} %reduce_sum.79), channel_id=1, replica_groups=mesh['sx'=8,'sz'=16] {'sx','sz'}, use_global_device_ids=true, to_apply=%region_8.9 | all-reduce | flops 64 | bytes 512 | tf_op jit(solution)/shard_map/psum | solution.py:62
  363.0 0.1 mul.95
  363.1 2.0 fusion.5
  365.4 35.6 %all_to_all.23 = f32[16,9,16,256]{3,2,1,0:T(8,128)S(1)} all-to-all(f32[16,9,16,256]{3,2,1,0:T(8,128)S(1)} %fusion.63), channel_id=1, replica_groups=mesh['sx'=8,'sz'=16] {'sz'}, dimensions={0} | all-to-all | bytes 4718592 | tf_op jit(solution)/shard_map/all_to_all | solution.py:76
  401.0 1.6 copy.99
  (37 shorter events, 0.3 us)
Async XLA Ops:
  0.0 128.9 %copy-start = (bf16[256,256]{1,0:T(8,128)(2,1)S(1)}, bf16[256,256]{1,0:T(8,128)(2,1)}, u32[]{:S(2)}) copy-start(bf16[256,256]{1,0:T(8,128)(2,1)} %param.9) | copy-start | bytes 393220
  36.9 40.4 %all-to-all-start = ((f32[16,1,36864]{2,1,0:T(1,128)}), f32[16,1,36864]{2,1,0:T(1,128)S(1)}, u32[]{:S(2)}, u32[]{:S(2)}) async-start(f32[16,1,36864]{2,1,0:T(1,128)} %reshape.83), calls=%async_computation | async-start | bytes 4718592 | tf_op jit(solution)/shard_map/all_to_all | solution.py:68
  77.3 1.4 copy-start.4
  127.4 1.5 copy-start.6
  127.4 1.5 copy-start.7
  132.2 5.9 %copy-start.5 = (s32[5]{0:T(128)S(1)}, s32[5]{0:T(128)}, u32[]{:S(2)}) copy-start(s32[5]{0:T(128)} %param.8) | copy-start | bytes 64
  134.6 33.8 %collective-permute-start = (bf16[6,256,256]{2,1,0:T(8,128)(2,1)}, bf16[6,256,256]{2,1,0:T(8,128)(2,1)}, u32[]{:S(2)}, u32[]{:S(2)}) collective-permute-start(bf16[6,256,256]{2,1,0:T(8,128)(2,1)} %get-tuple-element.15), channel_id=1, source_target_pairs={{0,16},{16,32},{32,48},{48,64},{64,80},{80,96},{96,112},{112,0},{1... | collective-permute-start | bytes 2359304 | tf_op jit(solution)/shard_map/ppermute | solution.py:21
  135.3 35.4 %collective-permute-start.1 = (bf16[6,256,256]{2,1,0:T(8,128)(2,1)S(1)}, bf16[6,256,256]{2,1,0:T(8,128)(2,1)}, u32[]{:S(2)}, u32[]{:S(2)}) collective-permute-start(bf16[6,256,256]{2,1,0:T(8,128)(2,1)S(1)} %get-tuple-element.16), channel_id=1, source_target_pairs={{16,0},{32,16},{48,32},{64,48},{80,64},{96,80},{112,96},{0,112},{1... | collective-permute-start | bytes 2359304 | tf_op jit(solution)/shard_map/ppermute | solution.py:22
  170.7 5.9 %slice-start = ((s8[5898240]{0:T(1024)(128)(4,1)}), s8[4194304]{0:T(1024)(128)(4,1)S(1)}, s32[]{:S(2)}) async-start(s8[5898240]{0:T(1024)(128)(4,1)} %bitcast.178), calls=%async_computation.2 | async-start | bytes 8388608
  172.9 3.7 slice-start.1
  177.0 1.3 copy-start.1
  252.9 40.3 %slice-start.2 = ((s8[5898240]{0:T(1024)(128)(4,1)}), s8[4194304]{0:T(1024)(128)(4,1)S(1)}, s32[]{:S(2)}) async-start(s8[5898240]{0:T(1024)(128)(4,1)} %bitcast.180), calls=%async_computation.4 | async-start | bytes 8388608
  254.5 33.4 %collective-permute-start.2 = (bf16[6,256,256]{2,1,0:T(8,128)(2,1)S(1)}, bf16[6,256,256]{2,1,0:T(8,128)(2,1)S(1)}, u32[]{:S(2)}, u32[]{:S(2)}) collective-permute-start(bf16[6,256,256]{2,1,0:T(8,128)(2,1)S(1)} %get-tuple-element.13), channel_id=1, source_target_pairs={{0,16},{16,32},{32,48},{48,64},{64,80},{80,96},{96,112},{112,0},{1... | collective-permute-start | bytes 2359304 | tf_op jit(solution)/shard_map/ppermute | solution.py:21
  254.8 38.3 %slice-start.3 = ((s8[5898240]{0:T(1024)(128)(4,1)}), s8[1703936]{0:T(1024)(128)(4,1)S(1)}, s32[]{:S(2)}) async-start(s8[5898240]{0:T(1024)(128)(4,1)} %bitcast.180), calls=%async_computation.5 | async-start | bytes 3407872
  254.8 35.0 %collective-permute-start.3 = (bf16[6,256,256]{2,1,0:T(8,128)(2,1)S(1)}, bf16[6,256,256]{2,1,0:T(8,128)(2,1)S(1)}, u32[]{:S(2)}, u32[]{:S(2)}) collective-permute-start(bf16[6,256,256]{2,1,0:T(8,128)(2,1)S(1)} %get-tuple-element.14), channel_id=1, source_target_pairs={{16,0},{32,16},{48,32},{64,48},{80,64},{96,80},{112,96},{0,112},{1... | collective-permute-start | bytes 2359304 | tf_op jit(solution)/shard_map/ppermute | solution.py:22
  294.1 1.3 copy-start.2
  294.1 2.0 copy-start.3
